TPU v7x, 256 devices: a whole 4x4x8 slice. The times are simulated.
256 devices in a mesh: tile: 64 (over y, x_hi, z), rcpt: 4 (over x_lo, core).
Axes of the slice: x: 4 (x_hi: 2, x_lo: 2; x = x_hi * 2 + x_lo), y: 4, z: 8, core: 2. Of those that a mesh axis runs over, the one named last changes fastest.
Arguments:
- adjoint_state: float32 [64, 16, 1024, 256], P('rcpt', None, 'tile'), may hold values from -6 to 6
- met_fields: bfloat16 [12, 3, 16, 1024, 256], P(None, None, 'rcpt', 'tile'), may hold values from -0.34960938 to 0.34960938
- forcing: bfloat16 [64, 1024, 256], P(None, 'tile'), may hold values from -6 to 6
- cluster_ids: int32 [64], P('rcpt'), may hold values from 0 to 63
- hour_index: int32 [2], replicated, may hold values from 0 to 11
Outputs:
- adjoint_out: float32 [64, 16, 1024, 256], P('rcpt', None, 'tile')
All inputs are finite; a program needn't handle non-finite values.
Results may differ from a plain program's by a relative error of at most 0.00035.
Values may be sent and summed in bfloat16 or wider, within the bound.
No kernel may reach another device: no remote copies, remote signals or barrier semaphores. Data moves between devices by JAX's collectives and lax.ppermute only.
A program may use at most 64 MiB of HBM per device.

v0:
```python
import jax
import jax.numpy as jnp
from jax import lax
from jax.sharding import PartitionSpec as P

STEPS = 2


def for_sending(x):

    def short(part):
        return part.astype(jnp.bfloat16) if part.dtype == jnp.float32 else part

    return jax.tree.map(short, x)


def passed_along(block, axis, distance):
    devices = range(lax.axis_size(axis))
    route = [((i - distance) % len(devices), i) for i in devices]
    return lax.ppermute(block, axis, route)


def interior(lam, winds, east, west):
    cx = winds[0].astype(jnp.float32)
    cy = winds[1].astype(jnp.float32)
    py = lam * jnp.maximum(cy, 0.0)
    my = lam * jnp.minimum(cy, 0.0)
    zero = jnp.zeros_like(py[..., :1])
    north = jnp.concatenate([py[..., 1:], zero], axis=3)
    south = jnp.concatenate([zero, my[..., :-1]], axis=3)
    return lam * (1.0 - jnp.abs(cx) - jnp.abs(cy)) + east - west + north - south


def horizontal_shift(lam, winds):
    cx = winds[0].astype(jnp.float32)
    px = lam * jnp.maximum(cx, 0.0)
    mx = lam * jnp.minimum(cx, 0.0)
    east_edge = passed_along(for_sending(px[:, :, :1]), "tile", -1)
    west_edge = passed_along(for_sending(mx[:, :, -1:]), "tile", 1)
    east = jnp.concatenate([px[:, :, 1:], east_edge], axis=2)
    west = jnp.concatenate([west_edge, mx[:, :, :-1]], axis=2)
    return interior(lam, winds, east, west)


def vertical(lam, mixing):
    coeff = 0.02 + 0.25 * jnp.abs(mixing.astype(jnp.float32))
    flux = coeff[:-1] * (lam[:, 1:] - lam[:, :-1])
    zero = jnp.zeros_like(flux[:, :1])
    return jnp.concatenate([flux, zero], axis=1) - jnp.concatenate([zero, flux], axis=1)


def finish(lam, flat, mixing, source_rows):
    state = flat + vertical(lam, mixing)
    return state.at[:, -1].add(source_rows)


def per_device(adjoint_state, met_fields, forcing, cluster_ids, hour_index):
    lam = adjoint_state
    clusters = forcing.shape[0]
    onehot = (cluster_ids[:, None] == jnp.arange(clusters, dtype=jnp.int32)[None, :]).astype(
        jnp.bfloat16
    )
    source_rows = jnp.dot(onehot, forcing.reshape(clusters, -1), preferred_element_type=jnp.float32)
    source_rows = source_rows.reshape(lam.shape[0], lam.shape[2], lam.shape[3])
    locals_list = [
        lax.dynamic_index_in_dim(met_fields, hour_index[step], 0, keepdims=False)
        for step in range(STEPS)
    ]
    for step in range(STEPS):
        metnow = lax.all_gather(locals_list[step], "rcpt", axis=1, tiled=True)
        lam_next = finish(lam, horizontal_shift(lam, metnow), metnow[2], source_rows)
        lam = lam_next
    return lam


def solution(mesh):
    placed = (
        P("rcpt", None, "tile", None),
        P(None, None, "rcpt", "tile", None),
        P(None, "tile", None),
        P("rcpt"),
        P(),
    )
    return jax.shard_map(
        per_device,
        mesh=mesh,
        in_specs=placed,
        out_specs=P("rcpt", None, "tile", None),
        check_vma=False,
    )
```

profile of v0, /device:TPU:1, one launch (start us, length us, event | category | flops | bytes accessed | tf_op | source)
XLA Modules:
  0.0 97.3 jit_solution(4686769854852998408)
XLA Ops:
  0.0 1.3 %fusion.32 = (s32[1]{0:T(128)}, s32[1]{0:T(128)}) fusion(s32[2]{0:T(128)} %param.13), kind=kLoop, calls=%fused_computation.69 | loop fusion | bytes 16 | tf_op jit(solution)/shard_map/slice | solution.py:66
  4.9 1.0 constant_dynamic-slice_fusion
  5.9 9.2 %all-gather = bf16[1,3,16,16,256]{4,3,2,1,0:T(8,128)(2,1)S(1)} all-gather(bf16[1,3,4,16,256]{4,3,2,1,0:T(8,128)(2,1)S(1)} %get-tuple-element.39), channel_id=2, replica_groups=mesh['tile'=64,'rcpt'=4] {'rcpt'}, dimensions={2}, use_global_device_ids=true | all-gather | bytes 491520 | tf_op jit(solution)/shard_map/all_gather | solution.py:70
  15.3 6.5 %fusion.31 = (f32[16,16,16,256]{3,0,2,1:T(8,128)S(1)}, f32[16,16,16,256]{3,0,2,1:T(8,128)S(1)}, f32[16,16,16,256]{3,0,2,1:T(8,128)S(1)}) fusion(f32[16,16,16,256]{3,2,1,0:T(8,128)} %param.9, f32[16,16,256]{2,1,0:T(8,128)S(1)} %get-tuple-element.47, f32[16,16,256]{2,1,0:T(8,128)S(1)} %get-tuple-element.50), kind=kLoop, calls=%fused_computation.68 | loop fusion | flops 2097152 | bytes 17301504 | tf_op args[0]
  21.8 0.7 slice.250
  22.7 0.7 slice.251
  23.4 8.6 %collective-permute-start = (bf16[16,16,1,256]{3,0,2,1:T(8,128)(2,1)}, bf16[16,16,1,256]{3,0,2,1:T(8,128)(2,1)}, u32[]{:S(2)}, u32[]{:S(2)}) collective-permute-start(bf16[16,16,1,256]{3,0,2,1:T(8,128)(2,1)} %slice.251), channel_id=1, source_target_pairs={{4,0},{8,4},{12,8},{16,12},{20,16},{24,20},{28,24},{32,28},{36,32}... | collective-permute-start | bytes 393224 | tf_op jit(solution)/shard_map/ppermute | solution.py:20
  32.0 2.3 %slice.182 = f32[16,16,15,256]{3,0,2,1:T(8,128)} slice(f32[16,16,16,256]{3,0,2,1:T(8,128)S(1)} %get-tuple-element.36), slice={[0:16], [0:16], [1:16], [0:256]} | slice | bytes 7864320 | tf_op jit(solution)/shard_map/slice | solution.py:40
  34.3 2.3 %slice.185 = f32[16,16,15,256]{3,0,2,1:T(8,128)} slice(f32[16,16,16,256]{3,0,2,1:T(8,128)S(1)} %get-tuple-element.37), slice={[0:16], [0:16], [0:15], [0:256]} | slice | bytes 7864320 | tf_op jit(solution)/shard_map/slice | solution.py:41
  36.6 6.7 %all-gather.1 = bf16[1,3,16,16,256]{4,3,2,1,0:T(8,128)(2,1)S(1)} all-gather(bf16[1,3,4,16,256]{4,3,2,1,0:T(8,128)(2,1)S(1)} %get-tuple-element.38), channel_id=3, replica_groups=mesh['tile'=64,'rcpt'=4] {'rcpt'}, dimensions={2}, use_global_device_ids=true | all-gather | bytes 491520 | tf_op jit(solution)/shard_map/all_gather | solution.py:70
  43.4 0.8 slice.187
  44.2 1.0 fusion.22
  45.2 0.9 slice.202
  46.1 2.5 %fusion.9 = f32[16,15,16,256]{3,0,2,1:T(8,128)} fusion(f32[16,16,16,256]{3,0,2,1:T(8,128)S(1)} %get-tuple-element.35, f32[15,16,256]{2,1,0:T(8,128)S(1)} %slice_bitcast_fusion.1), kind=kLoop, calls=%fused_computation.17 | loop fusion | flops 1966080 | bytes 12042240 | tf_op jit(solution)/shard_map/mul | solution.py:47
  48.6 3.0 %slice_multiply_fusion.3 = (f32[16,16,16,255]{3,0,2,1:T(8,128)S(1)}, f32[16,16,16,255]{3,0,2,1:T(8,128)S(1)}) fusion(f32[16,16,16,256]{3,0,2,1:T(8,128)S(1)} %get-tuple-element.35, f32[16,16,255]{2,1,0:T(8,128)} %slice.187, f32[16,16,255]{2,1,0:T(8,128)S(1)} %bitcast.53), kind=kLoop, calls=%fused_computation.3 | loop fusion | flops 2088960 | bytes 17233920 | tf_op jit(solution)/shard_map/mul | solution.py:26
  51.6 1.7 %slice_bitcast_fusion = f32[15,16,256]{2,1,0:T(8,128)} fusion(f32[1,16,16,256]{3,2,1,0:T(8,128)} %get-tuple-element.45), kind=kLoop, calls=%fused_computation.61 | loop fusion | bytes 491520 | tf_op jit(solution)/shard_map/slice | solution.py:47
  53.2 0.9 convert_element_type.54
  54.2 0.9 convert_element_type.53
  55.2 12.0 %fusion.3 = f32[16,16,16,256]{3,0,2,1:T(8,128)S(1)} fusion(f32[16,16,1,256]{3,0,2,1:T(8,128)S(1)} %convert_element_type.53, f32[16,16,15,256]{3,0,2,1:T(8,128)} %slice.182, f32[16,16,15,256]{3,0,2,1:T(8,128)} %slice.185, f32[16,16,1,256]{3,0,2,1:T(8,128)S(1)} %convert_element_type.54, f32[16,15,16,256]{3,0,2,1:T(8,128)} %fusion.9, ...), kind=kLoop, calls=%fused_computation.8 | loop fusion | flops 9437184 | bytes 29327360 | tf_op jit(solution)/shard_map/add | solution.py:53
  67.2 0.3 fusion.27
  67.5 0.9 broadcast_multiply_fusion
  68.4 0.7 slice.248
  69.1 1.2 %slice.249 = bf16[16,16,1,256]{3,0,2,1:T(8,128)(2,1)} slice(f32[16,16,16,256]{3,0,2,1:T(8,128)S(1)} %get-tuple-element.32), slice={[0:16], [0:16], [0:1], [0:256]} | slice | bytes 262144 | tf_op jit(solution)/shard_map/slice | solution.py:38
  70.3 1.6 %collective-permute-start.2 = (bf16[16,16,1,256]{3,0,2,1:T(8,128)(2,1)}, bf16[16,16,1,256]{3,0,2,1:T(8,128)(2,1)}, u32[]{:S(2)}, u32[]{:S(2)}) collective-permute-start(bf16[16,16,1,256]{3,0,2,1:T(8,128)(2,1)} %slice.249), channel_id=1, source_target_pairs={{4,0},{8,4},{12,8},{16,12},{20,16},{24,20},{28,24},{32,28},{36,32}... | collective-permute-start | bytes 393224 | tf_op jit(solution)/shard_map/ppermute | solution.py:20
  71.9 1.8 %slice_multiply_fusion.1 = (f32[16,16,16,255]{3,0,2,1:T(8,128)S(1)}, f32[16,16,16,255]{3,0,2,1:T(8,128)S(1)}) fusion(f32[16,16,16,256]{3,0,2,1:T(8,128)S(1)} %get-tuple-element.54, f32[16,16,255]{2,1,0:T(8,128)S(1)} %copy-done.3, f32[16,16,255]{2,1,0:T(8,128)S(1)} %bitcast.52), kind=kLoop, calls=%fused_computation.1 | loop fusion | flops 2088960 | bytes 17233920 | tf_op jit(solution)/shard_map/mul | solution.py:26
  73.7 3.6 %fusion.8 = f32[16,15,16,256]{3,0,2,1:T(8,128)} fusion(f32[16,16,16,256]{3,0,2,1:T(8,128)S(1)} %get-tuple-element.54, f32[15,16,256]{2,1,0:T(8,128)} %slice_bitcast_fusion), kind=kLoop, calls=%fused_computation.15 | loop fusion | flops 1966080 | bytes 12042240 | tf_op jit(solution)/shard_map/mul | solution.py:47
  77.4 2.3 %slice.200 = f32[16,16,15,256]{3,0,2,1:T(8,128)} slice(f32[16,16,16,256]{3,0,2,1:T(8,128)S(1)} %copy-done.2), slice={[0:16], [0:16], [0:15], [0:256]} | slice | bytes 7864320 | tf_op jit(solution)/shard_map/slice | solution.py:41
  79.7 2.3 %slice.197 = f32[16,16,15,256]{3,0,2,1:T(8,128)} slice(f32[16,16,16,256]{3,0,2,1:T(8,128)S(1)} %get-tuple-element.32), slice={[0:16], [0:16], [1:16], [0:256]} | slice | bytes 7864320 | tf_op jit(solution)/shard_map/slice | solution.py:40
  82.0 0.9 convert_element_type.58
  82.9 0.9 convert_element_type.59
  83.9 8.9 %fusion.7 = f32[16,16,16,256]{3,0,2,1:T(8,128)S(1)} fusion(f32[16,16,1,256]{3,0,2,1:T(8,128)S(1)} %convert_element_type.58, f32[16,16,15,256]{3,0,2,1:T(8,128)} %slice.197, f32[16,16,15,256]{3,0,2,1:T(8,128)} %slice.200, f32[16,16,1,256]{3,0,2,1:T(8,128)S(1)} %convert_element_type.59, f32[16,15,16,256]{3,0,2,1:T(8,128)} %fusion.8, ...), kind=kLoop, calls=%fused_computation.13 | loop fusion | flops 9437184 | bytes 29327360 | tf_op jit(solution)/shard_map/add | solution.py:53
  92.8 4.4 %copy.22 = f32[16,16,16,256]{3,2,1,0:T(8,128)} copy(f32[16,16,16,256]{3,0,2,1:T(8,128)S(1)} %fusion.26) | data formatting | bytes 8388608 | tf_op jit(solution)/shard_map/scatter-add | solution.py:54
  (25 shorter events, 0.6 us)
Async XLA Ops:
  22.5 30.7 %collective-permute-start.1 = (bf16[16,16,1,256]{3,0,2,1:T(8,128)(2,1)}, bf16[16,16,1,256]{3,0,2,1:T(8,128)(2,1)}, u32[]{:S(2)}, u32[]{:S(2)}) collective-permute-start(bf16[16,16,1,256]{3,0,2,1:T(8,128)(2,1)} %slice.250), channel_id=1, source_target_pairs={{252,0},{0,4},{4,8},{8,12},{12,16},{16,20},{20,24},{24,28},{28,32}... | collective-permute-start | bytes 393224 | tf_op jit(solution)/shard_map/ppermute | solution.py:20
  23.4 30.7 %collective-permute-start = (bf16[16,16,1,256]{3,0,2,1:T(8,128)(2,1)}, bf16[16,16,1,256]{3,0,2,1:T(8,128)(2,1)}, u32[]{:S(2)}, u32[]{:S(2)}) collective-permute-start(bf16[16,16,1,256]{3,0,2,1:T(8,128)(2,1)} %slice.251), channel_id=1, source_target_pairs={{4,0},{8,4},{12,8},{16,12},{20,16},{24,20},{28,24},{32,28},{36,32}... | collective-permute-start | bytes 393224 | tf_op jit(solution)/shard_map/ppermute | solution.py:20
  48.6 6.5 %copy-start = (f32[16,16,16,256]{3,2,1,0:T(8,128)S(1)}, f32[16,16,16,256]{3,2,1,0:T(8,128)}, u32[]{:S(2)}) copy-start(f32[16,16,16,256]{3,2,1,0:T(8,128)} %param.9) | copy-start | bytes 12582916
  55.1 12.0 %copy-start.6 = (bf16[64,16,256]{2,1,0:T(8,128)(2,1)S(1)}, bf16[64,16,256]{2,1,0:T(8,128)(2,1)}, u32[]{:S(2)}) copy-start(bf16[64,16,256]{2,1,0:T(8,128)(2,1)} %param.11) | copy-start | bytes 1572868
  55.1 12.0 %copy-start.7 = (s32[16]{0:T(128)S(1)}, s32[16]{0:T(128)}, u32[]{:S(2)}) copy-start(s32[16]{0:T(128)} %param.12) | copy-start | bytes 196
  55.1 12.3 %copy-start.4 = (f32[16,16,256]{2,1,0:T(8,128)S(1)}, f32[16,16,256]{2,1,0:T(8,128)}, u32[]{:S(2)}) copy-start(f32[16,16,256]{2,1,0:T(8,128)} %get-tuple-element.41) | copy-start | bytes 786436
  55.2 12.3 %copy-start.5 = (f32[16,16,256]{2,1,0:T(8,128)S(1)}, f32[16,16,256]{2,1,0:T(8,128)}, u32[]{:S(2)}) copy-start(f32[16,16,256]{2,1,0:T(8,128)} %get-tuple-element.44) | copy-start | bytes 786436
  67.5 4.5 %copy-start.3 = (f32[16,16,255]{2,1,0:T(8,128)S(1)}, f32[16,16,255]{2,1,0:T(8,128)}, u32[]{:S(2)}) copy-start(f32[16,16,255]{2,1,0:T(8,128)} %slice.202) | copy-start | bytes 783364
  68.4 3.5 %copy-start.1 = (f32[16,16,16,256]{3,0,2,1:T(8,128)}, f32[16,16,16,256]{3,0,2,1:T(8,128)S(1)}, u32[]{:S(2)}) copy-start(f32[16,16,16,256]{3,0,2,1:T(8,128)S(1)} %get-tuple-element.31) | copy-start | bytes 12582916
  70.3 11.7 %collective-permute-start.2 = (bf16[16,16,1,256]{3,0,2,1:T(8,128)(2,1)}, bf16[16,16,1,256]{3,0,2,1:T(8,128)(2,1)}, u32[]{:S(2)}, u32[]{:S(2)}) collective-permute-start(bf16[16,16,1,256]{3,0,2,1:T(8,128)(2,1)} %slice.249), channel_id=1, source_target_pairs={{4,0},{8,4},{12,8},{16,12},{20,16},{24,20},{28,24},{32,28},{36,32}... | collective-permute-start | bytes 393224 | tf_op jit(solution)/shard_map/ppermute | solution.py:20
  71.9 11.0 %collective-permute-start.3 = (bf16[16,16,1,256]{3,0,2,1:T(8,128)(2,1)}, bf16[16,16,1,256]{3,0,2,1:T(8,128)(2,1)}, u32[]{:S(2)}, u32[]{:S(2)}) collective-permute-start(bf16[16,16,1,256]{3,0,2,1:T(8,128)(2,1)} %slice.248), channel_id=1, source_target_pairs={{252,0},{0,4},{4,8},{8,12},{12,16},{16,20},{20,24},{24,28},{28,32}... | collective-permute-start | bytes 393224 | tf_op jit(solution)/shard_map/ppermute | solution.py:20
  73.7 3.6 %copy-start.2 = (f32[16,16,16,256]{3,0,2,1:T(8,128)S(1)}, f32[16,16,16,256]{3,0,2,1:T(8,128)}, u32[]{:S(2)}) copy-start(f32[16,16,16,256]{3,0,2,1:T(8,128)} %copy-done.1) | copy-start | bytes 12582916
where the time goes:
time: 97.6 us; the launch traced here: 97.3 us
  other arithmetic  44.2 us (45%)
  local copies, waits for them, and re-layouts  22.7 us (23%)
  blocking collectives  15.9 us (16%)
  starting transfers between devices  10.4 us (11%)
  between operations  3.85 us (4%)
    add x2, other arithmetic, finish(): state = flat + vertical(lam, mixing)  20.8 us
    all_gather x2, blocking collectives, per_device(): metnow = lax.all_gather(locals_list[step], 'rcpt', axis=1, tiled=True)  15.9 us
    ppermute x4, starting transfers between devices, passed_along(): return lax.ppermute(block, axis, route)  10.4 us
    unnamed x1, other arithmetic  6.53 us
    mul x2, other arithmetic, vertical(): flux = coeff[:-1] * (lam[:, 1:] - lam[:, :-1])  6.15 us
    mul x2, other arithmetic, interior(): py = lam * jnp.maximum(cy, 0.0)  4.77 us
    slice x2, local copies, waits for them, and re-layouts, horizontal_shift(): east = jnp.concatenate([px[:, :, 1:], east_edge], axis=2)  4.69 us
    slice x2, local copies, waits for them, and re-layouts, horizontal_shift(): west = jnp.concatenate([west_edge, mx[:, :, :-1]], axis=2)  4.56 us
  transfers between devices with their start and end apart: 4, of which 0 were waited for; matrix products, arithmetic and copies ran while one was open for 28% of the time, Pallas kernels for 0%

commit v1 on v0

--- a/solution.py
+++ b/solution.py
@@ -67,7 +67,10 @@
         for step in range(STEPS)
     ]
     for step in range(STEPS):
-        metnow = lax.all_gather(locals_list[step], "rcpt", axis=1, tiled=True)
+        metnow = jnp.concatenate(
+            lax.all_to_all(jnp.stack([locals_list[step]] * lax.axis_size("rcpt")), "rcpt", 0, 0),
+            axis=1,
+        )
         lam_next = finish(lam, horizontal_shift(lam, metnow), metnow[2], source_rows)
         lam = lam_next
     return lam

time: 97.6 us -> 102 us (1.045)
  starting transfers between devices: 10.4 us -> 14.7 us
  blocking collectives: 15.9 us -> 12 us
  other arithmetic: 44.2 us -> 46.6 us
  local copies, waits for them, and re-layouts: 22.7 us -> 24.2 us
    all_gather x2 -> x0, blocking collectives: 15.9 us -> none  [per_device(): metnow = lax.all_gather(locals_list[step], 'rcpt', axis=1, tiled=True)]
    all_to_all x0 -> x1, blocking collectives: none -> 12 us  [per_device(): lax.all_to_all(jnp.stack([locals_list[step]] * lax.axis_size('rcpt')), 'r...]
    all_to_all x0 -> x1, starting transfers between devices: none -> 4.47 us  [per_device(): lax.all_to_all(jnp.stack([locals_list[step]] * lax.axis_size('rcpt')), 'r...]
    slice x2, local copies, waits for them, and re-layouts: 4.69 us -> 7.08 us  [horizontal_shift(): east = jnp.concatenate([px[:, :, 1:], east_edge], axis=2)]
    mul x2, other arithmetic: 4.77 us -> 6.76 us  [interior(): py = lam * jnp.maximum(cy, 0.0)]
    slice x2, local copies, waits for them, and re-layouts: 1.73 us -> 0.25 us  [interior(): north = jnp.concatenate([py[..., 1:], zero], axis=3)]
    mul x2 -> x0, other arithmetic: 1.17 us -> none  [interior(): return lam * (1.0 - jnp.abs(cx) - jnp.abs(cy)) + east - west + north - south]
  transfers between devices with their start and end apart: 4 -> 5, of which waited for: 0 -> 0; matrix products, arithmetic and copies ran while one was open for 28% -> 36% of each run, Pallas kernels for 0% -> 0%
where the time goes in v1:
time: 102 us
  other arithmetic  46.6 us (46%)
  local copies, waits for them, and re-layouts  24.2 us (24%)
  starting transfers between devices  14.7 us (14%)
  blocking collectives  12 us (12%)
  between operations  4.07 us (4%)
    add x2, other arithmetic, finish(): state = flat + vertical(lam, mixing)  21.3 us
    all_to_all x1, blocking collectives, per_device(): lax.all_to_all(jnp.stack([locals_list[step]] * lax.axis_size('rcpt')), 'r...  12 us
    ppermute x4, starting transfers between devices, passed_along(): return lax.ppermute(block, axis, route)  10.2 us
    slice x2, local copies, waits for them, and re-layouts, horizontal_shift(): east = jnp.concatenate([px[:, :, 1:], east_edge], axis=2)  7.08 us
    mul x2, other arithmetic, interior(): py = lam * jnp.maximum(cy, 0.0)  6.76 us
    unnamed x1, other arithmetic  6.53 us
    mul x2, other arithmetic, vertical(): flux = coeff[:-1] * (lam[:, 1:] - lam[:, :-1])  6.15 us
    slice x2, local copies, waits for them, and re-layouts, horizontal_shift(): west = jnp.concatenate([west_edge, mx[:, :, :-1]], axis=2)  4.72 us
  transfers between devices with their start and end apart: 5, of which 0 were waited for; matrix products, arithmetic and copies ran while one was open for 36% of the time, Pallas kernels for 0%

profile of v1, /device:TPU:1, one launch (start us, length us, event | category | flops | bytes accessed | tf_op | source)
XLA Modules:
  0.0 101.8 jit_solution(1009813860522566629)
XLA Ops:
  0.0 1.3 %fusion.22 = (s32[1]{0:T(128)}, s32[1]{0:T(128)}) fusion(s32[2]{0:T(128)} %param.13), kind=kLoop, calls=%fused_computation.57 | loop fusion | bytes 16 | tf_op jit(solution)/shard_map/slice | solution.py:66
  5.1 1.0 dynamic-slice_bitcast_fusion
  6.1 12.0 %all_to_all.10 = bf16[4,3,4,16,256]{4,3,2,1,0:T(8,128)(2,1)S(1)} all-to-all(bf16[4,3,4,16,256]{4,3,2,1,0:T(8,128)(2,1)S(1)} %stack.4), channel_id=1, replica_groups=mesh['tile'=64,'rcpt'=4] {'rcpt'}, dimensions={0} | all-to-all | bytes 786432 | tf_op jit(solution)/shard_map/all_to_all | solution.py:71
  18.1 0.8 stack.5
  18.9 4.5 %all-to-all-start.1 = ((bf16[4,3,4,16,256]{4,3,2,1,0:T(8,128)(2,1)}), bf16[4,3,4,16,256]{4,3,2,1,0:T(8,128)(2,1)S(1)}, u32[]{:S(2)}, u32[]{:S(2)}) async-start(bf16[4,3,4,16,256]{4,3,2,1,0:T(8,128)(2,1)} %stack.5), calls=%async_computation.1 | async-start | bytes 786432 | tf_op jit(solution)/shard_map/all_to_all | solution.py:71
  23.3 0.2 fusion.13
  23.7 6.5 %fusion.21 = (f32[16,16,16,256]{3,0,2,1:T(8,128)S(1)}, f32[16,16,16,256]{3,0,2,1:T(8,128)S(1)}, f32[16,16,16,256]{3,0,2,1:T(8,128)S(1)}) fusion(f32[16,16,16,256]{3,2,1,0:T(8,128)} %param.9, f32[16,16,256]{2,1,0:T(8,128)S(1)} %bitcast.48, f32[16,16,256]{2,1,0:T(8,128)S(1)} %bitcast.49), kind=kLoop, calls=%fused_computation.56 | loop fusion | flops 2097152 | bytes 17301504 | tf_op args[0]
  30.3 0.7 slice.241
  31.0 1.2 %slice.240 = bf16[16,16,1,256]{3,0,2,1:T(8,128)(2,1)} slice(f32[16,16,16,256]{3,0,2,1:T(8,128)S(1)} %get-tuple-element.37), slice={[0:16], [0:16], [15:16], [0:256]} | slice | bytes 262144 | tf_op jit(solution)/shard_map/slice | solution.py:39
  32.3 8.7 %collective-permute-start = (bf16[16,16,1,256]{3,0,2,1:T(8,128)(2,1)}, bf16[16,16,1,256]{3,0,2,1:T(8,128)(2,1)}, u32[]{:S(2)}, u32[]{:S(2)}) collective-permute-start(bf16[16,16,1,256]{3,0,2,1:T(8,128)(2,1)} %slice.241), channel_id=1, source_target_pairs={{4,0},{8,4},{12,8},{16,12},{20,16},{24,20},{28,24},{32,28},{36,32}... | collective-permute-start | bytes 393224 | tf_op jit(solution)/shard_map/ppermute | solution.py:20
  41.0 5.0 %slice_multiply_fusion.3 = (f32[16,16,16,255]{3,0,2,1:T(8,128)}, f32[16,16,16,255]{3,0,2,1:T(8,128)}) fusion(f32[16,16,16,256]{3,0,2,1:T(8,128)S(1)} %get-tuple-element.35, f32[16,16,255]{2,1,0:T(8,128)S(1)} %slice.179, f32[16,16,255]{2,1,0:T(8,128)S(1)} %bitcast.47), kind=kLoop, calls=%fused_computation.3 | loop fusion | flops 2088960 | bytes 17233920 | tf_op jit(solution)/shard_map/mul | solution.py:26
  46.0 2.5 %fusion.9 = f32[16,15,16,256]{3,0,2,1:T(8,128)} fusion(f32[16,16,16,256]{3,0,2,1:T(8,128)S(1)} %get-tuple-element.35, f32[15,16,256]{2,1,0:T(8,128)S(1)} %slice.183), kind=kLoop, calls=%fused_computation.17 | loop fusion | flops 1966080 | bytes 12042240 | tf_op jit(solution)/shard_map/mul | solution.py:47
  48.5 0.2 fusion.15
  48.7 4.7 %slice.174 = f32[16,16,15,256]{3,0,2,1:T(8,128)} slice(f32[16,16,16,256]{3,0,2,1:T(8,128)} %copy-done.7), slice={[0:16], [0:16], [1:16], [0:256]} | slice | bytes 7864320 | tf_op jit(solution)/shard_map/slice | solution.py:40
  53.4 2.4 %slice.177 = f32[16,16,15,256]{3,0,2,1:T(8,128)} slice(f32[16,16,16,256]{3,0,2,1:T(8,128)S(1)} %copy-done.6), slice={[0:16], [0:16], [0:15], [0:256]} | slice | bytes 7864320 | tf_op jit(solution)/shard_map/slice | solution.py:41
  55.8 0.7 slice.198
  56.7 1.7 %convert_element_type.86 = f32[16,16,1,256]{3,0,2,1:T(8,128)S(1)} convert(bf16[16,16,1,256]{3,0,2,1:T(8,128)(2,1)} %collective-permute-done.1) | non-fusion elementwise | flops 65536 | bytes 393216 | tf_op jit(solution)/shard_map/convert_element_type | solution.py:41
  58.4 0.9 convert_element_type.85
  59.3 12.3 %fusion.3 = f32[16,16,16,256]{3,0,2,1:T(8,128)S(1)} fusion(f32[16,16,1,256]{3,0,2,1:T(8,128)S(1)} %convert_element_type.85, f32[16,16,15,256]{3,0,2,1:T(8,128)} %slice.174, f32[16,16,15,256]{3,0,2,1:T(8,128)} %slice.177, f32[16,16,1,256]{3,0,2,1:T(8,128)S(1)} %convert_element_type.86, f32[16,15,16,256]{3,0,2,1:T(8,128)} %fusion.9, ...), kind=kLoop, calls=%fused_computation.8 | loop fusion | flops 9437184 | bytes 29327360 | tf_op jit(solution)/shard_map/add | solution.py:53
  71.7 0.3 fusion.17
  72.0 0.9 broadcast_multiply_fusion
  72.9 0.8 slice.238
  73.7 1.2 %slice.239 = bf16[16,16,1,256]{3,0,2,1:T(8,128)(2,1)} slice(f32[16,16,16,256]{3,0,2,1:T(8,128)S(1)} %get-tuple-element.32), slice={[0:16], [0:16], [0:1], [0:256]} | slice | bytes 262144 | tf_op jit(solution)/shard_map/slice | solution.py:38
  74.8 1.5 %collective-permute-start.2 = (bf16[16,16,1,256]{3,0,2,1:T(8,128)(2,1)}, bf16[16,16,1,256]{3,0,2,1:T(8,128)(2,1)}, u32[]{:S(2)}, u32[]{:S(2)}) collective-permute-start(bf16[16,16,1,256]{3,0,2,1:T(8,128)(2,1)} %slice.239), channel_id=1, source_target_pairs={{4,0},{8,4},{12,8},{16,12},{20,16},{24,20},{28,24},{32,28},{36,32}... | collective-permute-start | bytes 393224 | tf_op jit(solution)/shard_map/ppermute | solution.py:20
  76.3 1.8 %slice_multiply_fusion.1 = (f32[16,16,16,255]{3,0,2,1:T(8,128)S(1)}, f32[16,16,16,255]{3,0,2,1:T(8,128)S(1)}) fusion(f32[16,16,16,256]{3,0,2,1:T(8,128)S(1)} %get-tuple-element.54, f32[16,16,255]{2,1,0:T(8,128)S(1)} %slice.194, f32[16,16,255]{2,1,0:T(8,128)S(1)} %bitcast.46), kind=kLoop, calls=%fused_computation.1 | loop fusion | flops 2088960 | bytes 17233920 | tf_op jit(solution)/shard_map/mul | solution.py:26
  78.1 3.6 %fusion.8 = f32[16,15,16,256]{3,0,2,1:T(8,128)} fusion(f32[16,16,16,256]{3,0,2,1:T(8,128)S(1)} %get-tuple-element.54, f32[15,16,256]{2,1,0:T(8,128)} %slice.198), kind=kLoop, calls=%fused_computation.15 | loop fusion | flops 1966080 | bytes 12042240 | tf_op jit(solution)/shard_map/mul | solution.py:47
  81.8 2.3 %slice.192 = f32[16,16,15,256]{3,0,2,1:T(8,128)} slice(f32[16,16,16,256]{3,0,2,1:T(8,128)S(1)} %copy-done.4), slice={[0:16], [0:16], [0:15], [0:256]} | slice | bytes 7864320 | tf_op jit(solution)/shard_map/slice | solution.py:41
  84.0 2.3 %slice.189 = f32[16,16,15,256]{3,0,2,1:T(8,128)} slice(f32[16,16,16,256]{3,0,2,1:T(8,128)S(1)} %get-tuple-element.32), slice={[0:16], [0:16], [1:16], [0:256]} | slice | bytes 7864320 | tf_op jit(solution)/shard_map/slice | solution.py:40
  86.4 0.9 convert_element_type.90
  87.3 0.9 convert_element_type.91
  88.3 9.0 %fusion.7 = f32[16,16,16,256]{3,0,2,1:T(8,128)S(1)} fusion(f32[16,16,1,256]{3,0,2,1:T(8,128)S(1)} %convert_element_type.90, f32[16,16,15,256]{3,0,2,1:T(8,128)} %slice.189, f32[16,16,15,256]{3,0,2,1:T(8,128)} %slice.192, f32[16,16,1,256]{3,0,2,1:T(8,128)S(1)} %convert_element_type.91, f32[16,15,16,256]{3,0,2,1:T(8,128)} %fusion.8, ...), kind=kLoop, calls=%fused_computation.13 | loop fusion | flops 9437184 | bytes 29327360 | tf_op jit(solution)/shard_map/add | solution.py:53
  97.4 4.4 %copy.31 = f32[16,16,16,256]{3,2,1,0:T(8,128)} copy(f32[16,16,16,256]{3,0,2,1:T(8,128)S(1)} %fusion.16) | data formatting | bytes 8388608 | tf_op jit(solution)/shard_map/scatter-add | solution.py:54
  (32 shorter events, 0.5 us)
Async XLA Ops:
  18.9 29.6 %all-to-all-start.1 = ((bf16[4,3,4,16,256]{4,3,2,1,0:T(8,128)(2,1)}), bf16[4,3,4,16,256]{4,3,2,1,0:T(8,128)(2,1)S(1)}, u32[]{:S(2)}, u32[]{:S(2)}) async-start(bf16[4,3,4,16,256]{4,3,2,1,0:T(8,128)(2,1)} %stack.5), calls=%async_computation.1 | async-start | bytes 786432 | tf_op jit(solution)/shard_map/all_to_all | solution.py:71
  30.3 15.7 %copy-start.5 = (f32[16,16,16,256]{3,0,2,1:T(8,128)}, f32[16,16,16,256]{3,0,2,1:T(8,128)S(1)}, u32[]{:S(2)}) copy-start(f32[16,16,16,256]{3,0,2,1:T(8,128)S(1)} %get-tuple-element.37) | copy-start | bytes 12582916
  30.3 15.7 %copy-start.7 = (f32[16,16,16,256]{3,0,2,1:T(8,128)}, f32[16,16,16,256]{3,0,2,1:T(8,128)S(1)}, u32[]{:S(2)}) copy-start(f32[16,16,16,256]{3,0,2,1:T(8,128)S(1)} %get-tuple-element.36) | copy-start | bytes 12582916
  32.2 24.5 %collective-permute-start.1 = (bf16[16,16,1,256]{3,0,2,1:T(8,128)(2,1)}, bf16[16,16,1,256]{3,0,2,1:T(8,128)(2,1)}, u32[]{:S(2)}, u32[]{:S(2)}) collective-permute-start(bf16[16,16,1,256]{3,0,2,1:T(8,128)(2,1)} %slice.240), channel_id=1, source_target_pairs={{252,0},{0,4},{4,8},{8,12},{12,16},{16,20},{20,24},{24,28},{28,32}... | collective-permute-start | bytes 393224 | tf_op jit(solution)/shard_map/ppermute | solution.py:20
  32.3 26.1 %collective-permute-start = (bf16[16,16,1,256]{3,0,2,1:T(8,128)(2,1)}, bf16[16,16,1,256]{3,0,2,1:T(8,128)(2,1)}, u32[]{:S(2)}, u32[]{:S(2)}) collective-permute-start(bf16[16,16,1,256]{3,0,2,1:T(8,128)(2,1)} %slice.241), channel_id=1, source_target_pairs={{4,0},{8,4},{12,8},{16,12},{20,16},{24,20},{28,24},{32,28},{36,32}... | collective-permute-start | bytes 393224 | tf_op jit(solution)/shard_map/ppermute | solution.py:20
  48.5 4.9 %copy-start.6 = (f32[16,16,16,256]{3,0,2,1:T(8,128)S(1)}, f32[16,16,16,256]{3,0,2,1:T(8,128)}, u32[]{:S(2)}) copy-start(f32[16,16,16,256]{3,0,2,1:T(8,128)} %copy-done.5) | copy-start | bytes 12582916
  48.6 10.7 %copy-start.2 = (f32[16,16,16,255]{3,0,2,1:T(8,128)S(1)}, f32[16,16,16,255]{3,0,2,1:T(8,128)}, u32[]{:S(2)}) copy-start(f32[16,16,16,255]{3,0,2,1:T(8,128)} %get-tuple-element.34) | copy-start | bytes 12533764
  53.4 5.9 %copy-start = (f32[16,16,16,256]{3,2,1,0:T(8,128)S(1)}, f32[16,16,16,256]{3,2,1,0:T(8,128)}, u32[]{:S(2)}) copy-start(f32[16,16,16,256]{3,2,1,0:T(8,128)} %param.9) | copy-start | bytes 12582916
  53.4 5.9 %copy-start.1 = (f32[16,16,16,255]{3,0,2,1:T(8,128)S(1)}, f32[16,16,16,255]{3,0,2,1:T(8,128)}, u32[]{:S(2)}) copy-start(f32[16,16,16,255]{3,0,2,1:T(8,128)} %get-tuple-element.33) | copy-start | bytes 12533764
  59.3 12.3 %copy-start.8 = (bf16[64,16,256]{2,1,0:T(8,128)(2,1)S(1)}, bf16[64,16,256]{2,1,0:T(8,128)(2,1)}, u32[]{:S(2)}) copy-start(bf16[64,16,256]{2,1,0:T(8,128)(2,1)} %param.11) | copy-start | bytes 1572868
  59.3 12.3 %copy-start.9 = (s32[16]{0:T(128)S(1)}, s32[16]{0:T(128)}, u32[]{:S(2)}) copy-start(s32[16]{0:T(128)} %param.12) | copy-start | bytes 196
  72.9 3.4 %copy-start.3 = (f32[16,16,16,256]{3,0,2,1:T(8,128)}, f32[16,16,16,256]{3,0,2,1:T(8,128)S(1)}, u32[]{:S(2)}) copy-start(f32[16,16,16,256]{3,0,2,1:T(8,128)S(1)} %get-tuple-element.31) | copy-start | bytes 12582916
  74.8 11.6 %collective-permute-start.2 = (bf16[16,16,1,256]{3,0,2,1:T(8,128)(2,1)}, bf16[16,16,1,256]{3,0,2,1:T(8,128)(2,1)}, u32[]{:S(2)}, u32[]{:S(2)}) collective-permute-start(bf16[16,16,1,256]{3,0,2,1:T(8,128)(2,1)} %slice.239), channel_id=1, source_target_pairs={{4,0},{8,4},{12,8},{16,12},{20,16},{24,20},{28,24},{32,28},{36,32}... | collective-permute-start | bytes 393224 | tf_op jit(solution)/shard_map/ppermute | solution.py:20
  76.3 11.0 %collective-permute-start.3 = (bf16[16,16,1,256]{3,0,2,1:T(8,128)(2,1)}, bf16[16,16,1,256]{3,0,2,1:T(8,128)(2,1)}, u32[]{:S(2)}, u32[]{:S(2)}) collective-permute-start(bf16[16,16,1,256]{3,0,2,1:T(8,128)(2,1)} %slice.238), channel_id=1, source_target_pairs={{252,0},{0,4},{4,8},{8,12},{12,16},{16,20},{20,24},{24,28},{28,32}... | collective-permute-start | bytes 393224 | tf_op jit(solution)/shard_map/ppermute | solution.py:20
  78.1 3.6 %copy-start.4 = (f32[16,16,16,256]{3,0,2,1:T(8,128)S(1)}, f32[16,16,16,256]{3,0,2,1:T(8,128)}, u32[]{:S(2)}) copy-start(f32[16,16,16,256]{3,0,2,1:T(8,128)} %copy-done.3) | copy-start | bytes 12582916
